TPU v7x, 32 devices: a whole 2x2x4 slice. The times are simulated.
32 devices in a mesh: groups: 2 (over x), psg: 16 (over z, y, core).
Axes of the slice: x: 2, y: 2, z: 4, core: 2. Of those that a mesh axis runs over, the one named last changes fastest.
Arguments:
- queries: bfloat16 [64, 32, 128], P(('groups', 'psg')), parts along dimension 0, may hold values from -0.29882812 to 0.29882812
- candidates: int32 [64, 512], P(('groups', 'psg')), parts along dimension 0, may hold values from 0 to 159
- centroids: bfloat16 [8192, 128], P('psg'), may hold values from -6 to 6
- bucket_weights: float32 [4, 128], replicated, may hold values from -1 to 1
- centroid_shard: int32 [32768, 1], P('psg'), may hold values from 0 to 15; in each aligned block of 2048 rows (0 to 2047, 2048 to 4095, ...) at most 256 rows name the same one
- centroid_row: int32 [32768], P('psg'), may hold values from 0 to 511
- residual_codes: int32 [32768, 128], P('psg'), may hold values from 0 to 3
- tile_count: int32 [160], replicated, may hold values from 1 to 3, 256 in all
- last_fill: int32 [160], replicated, may hold values from 1 to 128
Outputs:
- scores: float32 [64, 512], P(('groups', 'psg')), parts along dimension 0
There are 2 independent parts, one for each index of `groups`. A program takes and returns all parts, laid end to end along the dimension named above; an argument that names none is the same for every part. Nothing has to cross between parts.
Inputs may be any that keep to these rules, and one draw needn't show every extreme that they name: `tile_count`: tiles are numbered along psg, device k holding tiles k * 16 onward; the counts sum to 256, so a passage may continue on the next device. `centroid_shard`: among the 2048 token slots of one device, at most 256 name the same device; on some device some value is named exactly 256 times.
All inputs are finite; a program needn't handle non-finite values.
Results may differ from a plain program's by a relative error of at most 0.0003.
Values may be sent and summed in bfloat16 or wider, within the bound.
No kernel may reach another device: no remote copies, remote signals or barrier semaphores. Data moves between devices by JAX's collectives and lax.ppermute only.
A program may use at most 64 MiB of HBM per device.

v0:
```python
import functools

import jax
import jax.numpy as jnp
from jax import lax
from jax.experimental import pallas as pl
from jax.experimental.pallas import tpu as pltpu
from jax.sharding import PartitionSpec as P


TILE = 128
LANES = 128
EPSILON = 1e-06
GRANT = 8 << 20


def swap(x, offset):
    n = lax.axis_size("psg")
    return lax.ppermute(x, "psg", [(i, i ^ offset) for i in range(n)])


def bits_of(n):
    return [1 << k for k in reversed(range(n.bit_length() - 1))]


def spread(own, beside):
    bits = bits_of(lax.axis_size("psg"))
    far, mid, low = bits[0], bits[1], bits[2]
    held = {0: own}
    held[far] = swap(own, far)
    held[low] = swap(own, low)
    held[mid ^ low] = swap(own, mid ^ low)
    held[mid] = swap(own, mid)
    held[far ^ low] = swap(held[far], low)
    held[far ^ mid ^ low] = swap(held[far], mid ^ low)
    held[far ^ mid] = swap(held[far], mid)
    held[far ^ low], beside = lax.optimization_barrier((held[far ^ low], beside))
    pieces = [((o,), array) for o, array in held.items()]
    for bit in bits[3:]:
        if len(pieces) > 8:
            pieces = [(sum([o for o, _ in pieces], ()), jnp.concatenate([a for _, a in pieces]))]
        pieces = pieces + [(tuple(o ^ bit for o in names), swap(array, bit)) for names, array in pieces]
    return pieces, beside


def passages(count_ref):
    count = count_ref[...]
    before = lax.broadcasted_iota(jnp.int32, (LANES, LANES), 0) < lax.broadcasted_iota(jnp.int32, (LANES, LANES), 1)
    within = jnp.dot(
        count.astype(jnp.float32).astype(jnp.bfloat16),
        jnp.where(before, 1.0, 0.0).astype(jnp.bfloat16),
        preferred_element_type=jnp.float32,
    ).astype(jnp.int32)
    sums = jnp.sum(count, axis=1, keepdims=True)
    passed = jnp.zeros((1, 1), jnp.int32)
    spans = []
    for b in range(count.shape[0]):
        held = count[b : b + 1, :]
        start = within[b : b + 1, :] + passed
        passed = passed + sums[b : b + 1, :]
        spans.append((start, jnp.where(held > 0, start + held - 1, -1)))
    return spans


def fill_kernel(place_ref, count_ref, last_ref, fill_ref):
    rows = fill_ref.shape[0]
    tile = lax.broadcasted_iota(jnp.int32, (rows, LANES), 0) + place_ref[0] * rows
    total = jnp.zeros((rows, LANES), jnp.int32)
    for b, (_, last) in enumerate(passages(count_ref)):
        total = total + jnp.where(tile == last, last_ref[b : b + 1, :] - TILE, 0)
    fill_ref[...] = jnp.broadcast_to(jnp.sum(total, axis=1, keepdims=True), (rows, LANES)) + TILE


def start_kernel(count_ref, start_ref, more_ref):
    spans = passages(count_ref)
    for b, (start, _) in enumerate(spans):
        start_ref[b : b + 1, :] = start

    def chunk(step, carry):
        first = pl.multiple_of(step * LANES, LANES)
        tile = lax.broadcasted_iota(jnp.int32, (LANES, LANES), 0) + first
        total = jnp.zeros((LANES, LANES), jnp.int32)
        for start, last in spans:
            total = total + jnp.where((start <= tile) & (tile <= last), last - tile, 0)
        more_ref[pl.ds(first, LANES), :] = jnp.broadcast_to(jnp.sum(total, axis=1, keepdims=True), (LANES, LANES))
        return carry

    lax.fori_loop(0, more_ref.shape[0] // LANES, chunk, 0)


def in_blocks(values):
    blocks = -(-values.shape[0] // LANES)
    return jnp.pad(values, (0, blocks * LANES - values.shape[0])).reshape(blocks, LANES)


def own_fill(place, counts, lasts, tiles_dev):
    vmem = pl.BlockSpec(memory_space=pltpu.VMEM)
    return pl.pallas_call(
        fill_kernel,
        out_shape=jax.ShapeDtypeStruct((tiles_dev, LANES), jnp.int32),
        in_specs=[pl.BlockSpec(memory_space=pltpu.SMEM), vmem, vmem],
        out_specs=vmem,
        compiler_params=pltpu.CompilerParams(vmem_limit_bytes=GRANT),
        name="own_fill",
    )(place, counts, lasts)


def tile_starts(counts, total_tiles):
    vmem = pl.BlockSpec(memory_space=pltpu.VMEM)
    return pl.pallas_call(
        start_kernel,
        out_shape=(
            jax.ShapeDtypeStruct(counts.shape, jnp.int32),
            jax.ShapeDtypeStruct((-(-total_tiles // LANES) * LANES, LANES), jnp.int32),
        ),
        in_specs=[vmem],
        out_specs=(vmem, vmem),
        compiler_params=pltpu.CompilerParams(vmem_limit_bytes=GRANT),
        name="tile_starts",
    )(counts)


def maxima_kernel(names, query_rows, place_ref, code_ref, fill_ref, residual_ref, *rest):
    pieces = rest[: len(names)]
    out_ref, book_ref, query_ref, even_ref, odd_ref, embedded_ref = rest[len(names) :]
    index = place_ref[0]
    each = pieces[0].shape[0] // len(names[0])
    cent_dev = each - query_rows
    for offsets, piece in zip(names, pieces):
        for k, offset in enumerate(offsets):
            book_at = pl.multiple_of((index ^ offset) * cent_dev, cent_dev)
            query_at = pl.multiple_of((index ^ offset) * query_rows, query_rows)
            query_ref[pl.ds(query_at, query_rows), :] = piece[k * each + cent_dev : (k + 1) * each, :]

            def expand(step, carry, piece=piece, start=k * each, book_at=book_at):
                at = pl.multiple_of(step * LANES, LANES)
                rows = piece[pl.ds(start + at, LANES), :].astype(jnp.float32)
                book_ref[pl.ds(book_at + at, LANES), :] = rows
                return carry

            lax.fori_loop(0, cent_dev // LANES, expand, 0, unroll=len(names) > 8)

    tiles = residual_ref.shape[0] // TILE
    slot = lax.broadcasted_iota(jnp.int32, (TILE, LANES), 0)

    def pick(tile, into):
        base = tile * TILE
        for u in range(TILE):
            into[u : u + 1, :] = book_ref[pl.ds(code_ref[base + u], 1), :]

    def decode(tile, picked):
        rows = pl.ds(pl.multiple_of(tile * TILE, TILE), TILE)
        summed = picked[...] + residual_ref[rows, :]
        scale = lax.rsqrt(jnp.sum(summed * summed, axis=1, keepdims=True) + EPSILON)
        embedded = summed * scale
        embedded = jnp.where(slot < fill_ref[pl.ds(tile, 1), :], embedded, embedded[0:1, :])
        embedded_ref[rows, :] = embedded.astype(jnp.bfloat16)

    pick(0, even_ref)

    def pair(step, carry):
        tile = 2 * step
        pick(tile + 1, odd_ref)
        decode(tile, even_ref)
        pick(jnp.minimum(tile + 2, tiles - 1), even_ref)
        decode(tile + 1, odd_ref)
        return carry

    lax.fori_loop(0, tiles // 2, pair, 0)

    width = 2 * LANES
    per = LANES // query_rows
    deep = tiles // per
    lane = lax.broadcasted_iota(jnp.int32, (deep, LANES), 1)

    def score(step, carry):
        q = query_ref[pl.ds(pl.multiple_of(step * width, width), width), :]
        rows = []
        for t in range(tiles):
            products = lax.dot_general(
                embedded_ref[t * TILE : (t + 1) * TILE, :],
                q,
                (((1,), (1,)), ((), ())),
                preferred_element_type=jnp.float32,
            )
            rows.append(jnp.max(products, axis=0, keepdims=True))
        best = jnp.concatenate(rows, axis=0)
        for b in range(width // LANES):
            block = best[:, b * LANES : (b + 1) * LANES]
            for turn in range(per):
                made = None
                for g in range(per):
                    part = block[g * deep : (g + 1) * deep, :]
                    shift = (g - turn) * query_rows % LANES
                    if shift:
                        part = pltpu.roll(part, shift, 1)
                    made = part if made is None else jnp.where(lane < g * query_rows, made, part)
                out_ref[step * (width // query_rows) + b * per + turn] = made
        return carry

    lax.fori_loop(0, query_ref.shape[0] // width, score, 0)


def tile_maxima(held, place, codes, fill, residual, query_rows):
    n = lax.axis_size("psg")
    tokens, dim = residual.shape
    cent_dev = held[0][1].shape[0] // len(held[0][0]) - query_rows
    per = LANES // query_rows
    smem = pl.BlockSpec(memory_space=pltpu.SMEM)
    vmem = pl.BlockSpec(memory_space=pltpu.VMEM)
    names = tuple(o for o, _ in held)
    room = (n * (cent_dev * 6 + query_rows * 4) + tokens * 6) * dim + GRANT
    return pl.pallas_call(
        functools.partial(maxima_kernel, names, query_rows),
        out_shape=jax.ShapeDtypeStruct((n, tokens // TILE // per, LANES), jnp.float32),
        in_specs=[smem, smem, vmem, vmem] + [vmem] * len(held),
        out_specs=vmem,
        scratch_shapes=[
            pltpu.VMEM((n * cent_dev, dim), jnp.float32),
            pltpu.VMEM((n * query_rows, dim), jnp.bfloat16),
            pltpu.VMEM((TILE, dim), jnp.float32),
            pltpu.VMEM((TILE, dim), jnp.float32),
            pltpu.VMEM((tokens, dim), jnp.bfloat16),
        ],
        compiler_params=pltpu.CompilerParams(vmem_limit_bytes=room),
        name="tile_maxima",
    )(place, codes, fill, residual, *[a for _, a in held])


def lookup(table, rows_of):
    within = rows_of & (LANES - 1)
    block = rows_of >> 7
    found = None
    for b, values in enumerate(table):
        got = jnp.take_along_axis(values, within, axis=1, mode="promise_in_bounds")
        found = got if found is None else jnp.where(block == b, got, found)
    return found


def assemble_kernel(query_len, maxima_ref, more_ref, start_ref, candidate_ref, out_ref, tiles_ref):
    n, deep, _ = maxima_ref.shape
    queries, candidates = candidate_ref.shape
    query_rows = queries * query_len
    per = LANES // query_rows
    total = n * deep * per
    for j in range(n):
        got = maxima_ref[j]
        for g in range(per):
            at = (j * per + g) * deep
            part = got if g == 0 else pltpu.roll(got, LANES - g * query_rows, 1)
            tiles_ref[at : at + deep, :] = part
    tiles_ref[total : total + 8, :] = jnp.zeros((8, LANES), jnp.float32)
    more = more_ref[0:total, :]
    combined = tiles_ref[0:total, :]
    combined = jnp.maximum(combined, jnp.where(more >= 1, tiles_ref[1 : total + 1, :], combined))
    combined = jnp.maximum(combined, jnp.where(more >= 2, tiles_ref[2 : total + 2, :], combined))
    chunks = candidates // LANES
    row = lax.broadcasted_iota(jnp.int32, (8, LANES), 0)
    lane = lax.broadcasted_iota(jnp.int32, (8, LANES), 1)
    high = combined.astype(jnp.bfloat16)
    left = combined - high.astype(jnp.float32)
    middle = left.astype(jnp.bfloat16)
    low = (left - middle.astype(jnp.float32)).astype(jnp.bfloat16)
    groups = [(q, c) for q in range(queries) for c in range(chunks)]
    for first in range(0, len(groups), 8):
        some = groups[first : first + 8]
        owner = jnp.zeros((8, LANES), jnp.int32)
        wanted = jnp.zeros((8, LANES), jnp.int32)
        for r, (q, c) in enumerate(some):
            owner = jnp.where(row == r, q, owner)
            ids = candidate_ref[q : q + 1, c * LANES : (c + 1) * LANES]
            wanted = jnp.where(row == r, ids, wanted)
        select = jnp.where((lane >= owner * query_len) & (lane < (owner + 1) * query_len), 1.0, 0.0).astype(jnp.bfloat16)
        sums = None
        for part in (low, middle, high):
            term = lax.dot_general(select, part, (((1,), (1,)), ((), ())), preferred_element_type=jnp.float32)
            sums = term if sums is None else sums + term
        starts = [
            jnp.broadcast_to(start_ref[b : b + 1, :], (8, LANES)) for b in range(start_ref.shape[0])
        ]
        first_tile = lookup(starts, wanted)
        found = lookup([sums[:, b * LANES : (b + 1) * LANES] for b in range(-(-total // LANES))], first_tile)
        for r, (q, c) in enumerate(some):
            out_ref[q : q + 1, c * LANES : (c + 1) * LANES] = found[r : r + 1, :]


def assemble(own_maxima, more, starts, candidates, query_len):
    n, deep, _ = own_maxima.shape
    per = LANES // (candidates.shape[0] * query_len)
    total = n * deep * per
    vmem = pl.BlockSpec(memory_space=pltpu.VMEM)
    return pl.pallas_call(
        functools.partial(assemble_kernel, query_len),
        out_shape=jax.ShapeDtypeStruct(candidates.shape, jnp.float32),
        in_specs=[vmem] * 4,
        out_specs=vmem,
        scratch_shapes=[pltpu.VMEM((total + 8, LANES), jnp.float32)],
        compiler_params=pltpu.CompilerParams(vmem_limit_bytes=GRANT),
        name="assemble",
    )(own_maxima, more, starts, candidates)


def per_device(
    queries,
    candidates,
    centroids,
    bucket_weights,
    centroid_shard,
    centroid_row,
    residual_codes,
    tile_count,
    last_fill,
):
    n = lax.axis_size("psg")
    place = lax.axis_index("psg").astype(jnp.int32).reshape(1)
    num_queries, query_len, dim = queries.shape
    tiles_dev = residual_codes.shape[0] // TILE
    counts, lasts = in_blocks(tile_count), in_blocks(last_fill)
    codes = centroid_shard[:, 0] * centroids.shape[0] + centroid_row
    residual = jnp.where(
        residual_codes < 2,
        jnp.where(residual_codes == 0, bucket_weights[0], bucket_weights[1]),
        jnp.where(residual_codes == 2, bucket_weights[2], bucket_weights[3]),
    )
    fill = own_fill(place, counts, lasts, tiles_dev)
    query_rows = num_queries * query_len
    own = jnp.concatenate([centroids, queries.reshape(query_rows, dim)])
    held, (codes, fill, counts, residual) = spread(own, (codes, fill, counts, residual))
    maxima = tile_maxima(held, place, codes, fill, residual, query_rows)
    maxima, counts = lax.optimization_barrier((maxima, counts))
    starts, more = tile_starts(counts, tiles_dev * n)
    own_maxima = lax.all_to_all(maxima, "psg", split_axis=0, concat_axis=0, tiled=True)
    return assemble(own_maxima, more, starts, candidates, query_len)


def solution(mesh):
    placed = (
        P(("groups", "psg"), None, None),
        P(("groups", "psg"), None),
        P("psg", None),
        P(),
        P("psg", None),
        P("psg"),
        P("psg", None),
        P(),
        P(),
    )
    return jax.shard_map(
        per_device,
        mesh=mesh,
        in_specs=placed,
        out_specs=P(("groups", "psg"), None),
        check_vma=False,
    )
```

profile of v0, /device:TPU:0, one launch (start us, length us, event | category | flops | bytes accessed | tf_op | source)
XLA Modules:
  0.0 47.0 jit_solution(17552540079122565435)
XLA Ops:
  0.0 0.9 %pad_maximum_fusion.rest_0_ = bf16[576,128]{1,0:T(8,128)(2,1)S(1)} fusion(bf16[64,128]{1,0:T(8,128)(2,1)} %bitcast.16, bf16[512,128]{1,0:T(8,128)(2,1)} %param.11), kind=kLoop, calls=%fused_computation.1 | loop fusion | flops 294912 | bytes 294912 | tf_op jit(solution)/shard_map/concatenate | solution.py:327
  1.0 0.6 %collective-permute-start.7 = (bf16[576,128]{1,0:T(8,128)(2,1)S(1)}, bf16[576,128]{1,0:T(8,128)(2,1)S(1)}, u32[]{:S(2)}, u32[]{:S(2)}) collective-permute-start(bf16[576,128]{1,0:T(8,128)(2,1)S(1)} %pad_maximum_fusion.rest_0_), channel_id=1, source_target_pairs={{0,1},{1,0},{2,3},{3,2},{4,5},{5,4},{6,7},{7,6},{8,9},{9,8},{10,11... | collective-permute-start | bytes 442376 | tf_op jit(solution)/shard_map/ppermute | solution.py:19
  1.5 2.6 %collective-permute-start.4 = (bf16[576,128]{1,0:T(8,128)(2,1)S(1)}, bf16[576,128]{1,0:T(8,128)(2,1)S(1)}, u32[]{:S(2)}, u32[]{:S(2)}) collective-permute-start(bf16[576,128]{1,0:T(8,128)(2,1)S(1)} %pad_maximum_fusion.rest_0_), channel_id=1, source_target_pairs={{0,4},{1,5},{2,6},{3,7},{4,0},{5,1},{6,2},{7,3},{8,12},{9,13},{10,... | collective-permute-start | bytes 442376 | tf_op jit(solution)/shard_map/ppermute | solution.py:19
  4.1 1.4 %collective-permute-start.3 = (bf16[576,128]{1,0:T(8,128)(2,1)S(1)}, bf16[576,128]{1,0:T(8,128)(2,1)S(1)}, u32[]{:S(2)}, u32[]{:S(2)}) collective-permute-start(bf16[576,128]{1,0:T(8,128)(2,1)S(1)} %pad_maximum_fusion.rest_0_), channel_id=1, source_target_pairs={{0,6},{1,7},{2,4},{3,5},{4,2},{5,3},{6,0},{7,1},{8,14},{9,15},{10,... | collective-permute-start | bytes 442376 | tf_op jit(solution)/shard_map/ppermute | solution.py:19
  5.7 3.0 %collective-permute-start = (bf16[576,128]{1,0:T(8,128)(2,1)S(1)}, bf16[576,128]{1,0:T(8,128)(2,1)S(1)}, u32[]{:S(2)}, u32[]{:S(2)}) collective-permute-start(bf16[576,128]{1,0:T(8,128)(2,1)S(1)} %pad_maximum_fusion.rest_0_), channel_id=1, source_target_pairs={{0,8},{1,9},{2,10},{3,11},{4,12},{5,13},{6,14},{7,15},{8,0},{9,1},... | collective-permute-start | bytes 442376 | tf_op jit(solution)/shard_map/ppermute | solution.py:19
  8.7 5.6 %collective-permute-done.rest_1_ = bf16[576,128]{1,0:T(8,128)(2,1)S(1)} collective-permute-done((bf16[576,128]{1,0:T(8,128)(2,1)S(1)}, bf16[576,128]{1,0:T(8,128)(2,1)S(1)}, u32[]{:S(2)}, u32[]{:S(2)}) %collective-permute-start) | collective-permute-done | bytes 147488 | tf_op jit(solution)/shard_map/ppermute | solution.py:19
  14.3 1.5 %collective-permute-start.1 = (bf16[576,128]{1,0:T(8,128)(2,1)S(1)}, bf16[576,128]{1,0:T(8,128)(2,1)S(1)}, u32[]{:S(2)}, u32[]{:S(2)}) collective-permute-start(bf16[576,128]{1,0:T(8,128)(2,1)S(1)} %collective-permute-done.rest_1_), channel_id=1, source_target_pairs={{0,2},{1,3},{2,0},{3,1},{4,6},{5,7},{6,4},{7,5},{8,10},{9,11},{10,... | collective-permute-start | bytes 442376 | tf_op jit(solution)/shard_map/ppermute | solution.py:19
  15.8 1.4 %select_select_fusion.residual_ref = f32[2048,128]{1,0:T(8,128)S(1)} fusion(s32[2048,128]{1,0:T(8,128)} %param.15, f32[128]{0:T(128)S(1)} %get-tuple-element.25, f32[128]{0:T(128)S(1)} %get-tuple-element.26, f32[128]{0:T(128)S(1)} %get-tuple-element.24, f32[128]{0:T(128)S(1)} %get-tuple-element.23), kind=kLoop, calls=%fused_computation | loop fusion | flops 1572864 | bytes 2099200 | tf_op jit(solution)/shard_map/jit(_where)/select_n | solution.py:320
  17.3 3.5 %collective-permute-start.6 = (bf16[576,128]{1,0:T(8,128)(2,1)S(1)}, bf16[576,128]{1,0:T(8,128)(2,1)S(1)}, u32[]{:S(2)}, u32[]{:S(2)}) collective-permute-start(bf16[576,128]{1,0:T(8,128)(2,1)S(1)} %collective-permute-done.rest_1_), channel_id=1, source_target_pairs={{0,4},{1,5},{2,6},{3,7},{4,0},{5,1},{6,2},{7,3},{8,12},{9,13},{10,... | collective-permute-start | bytes 442376 | tf_op jit(solution)/shard_map/ppermute | solution.py:19
  20.9 0.5 %collective-permute-start.10 = (bf16[576,128]{1,0:T(8,128)(2,1)S(1)}, bf16[576,128]{1,0:T(8,128)(2,1)S(1)}, u32[]{:S(2)}, u32[]{:S(2)}) collective-permute-start(bf16[576,128]{1,0:T(8,128)(2,1)S(1)} %collective-permute-done.3.rest_3_), channel_id=1, source_target_pairs={{0,1},{1,0},{2,3},{3,2},{4,5},{5,4},{6,7},{7,6},{8,9},{9,8},{10,11... | collective-permute-start | bytes 442376 | tf_op jit(solution)/shard_map/ppermute | solution.py:19
  21.4 0.6 %copy-done.4 = s32[160]{0:T(256)S(1)} copy-done((s32[160]{0:T(256)S(1)}, s32[160]{0:T(256)}, u32[]{:S(2)}) %copy-start.4) | copy-done | bytes 664
  22.1 0.2 own_fill.1.fill_ref
  22.3 0.1 collective-permute-start.8
  22.5 0.4 collective-permute-start.9
  22.9 2.6 %collective-permute-done.6.rest_7_ = bf16[576,128]{1,0:T(8,128)(2,1)S(1)} collective-permute-done((bf16[576,128]{1,0:T(8,128)(2,1)S(1)}, bf16[576,128]{1,0:T(8,128)(2,1)S(1)}, u32[]{:S(2)}, u32[]{:S(2)}) %collective-permute-start.6) | collective-permute-done | bytes 147488 | tf_op jit(solution)/shard_map/ppermute | solution.py:19
  25.5 1.7 %collective-permute-done.5.rest_6_ = bf16[576,128]{1,0:T(8,128)(2,1)S(1)} collective-permute-done((bf16[576,128]{1,0:T(8,128)(2,1)S(1)}, bf16[576,128]{1,0:T(8,128)(2,1)S(1)}, u32[]{:S(2)}, u32[]{:S(2)}) %collective-permute-start.5) | collective-permute-done | bytes 147488 | tf_op jit(solution)/shard_map/ppermute | solution.py:19
  27.2 0.5 %collective-permute-start.12 = (bf16[576,128]{1,0:T(8,128)(2,1)S(1)}, bf16[576,128]{1,0:T(8,128)(2,1)S(1)}, u32[]{:S(2)}, u32[]{:S(2)}) collective-permute-start(bf16[576,128]{1,0:T(8,128)(2,1)S(1)} %collective-permute-done.1.rest_5_), channel_id=1, source_target_pairs={{0,1},{1,0},{2,3},{3,2},{4,5},{5,4},{6,7},{7,6},{8,9},{9,8},{10,11... | collective-permute-start | bytes 442376 | tf_op jit(solution)/shard_map/ppermute | solution.py:19
  27.7 0.8 %collective-permute-done.13.rest_14_ = bf16[576,128]{1,0:T(8,128)(2,1)S(1)} collective-permute-done((bf16[576,128]{1,0:T(8,128)(2,1)S(1)}, bf16[576,128]{1,0:T(8,128)(2,1)S(1)}, u32[]{:S(2)}, u32[]{:S(2)}) %collective-permute-start.13) | collective-permute-done | bytes 147488 | tf_op jit(solution)/shard_map/ppermute | solution.py:19
  28.5 0.2 collective-permute-done.12.rest_13_
  28.8 6.3 %tile_maxima.1 = f32[16,8,128]{2,1,0:T(8,128)} custom-call(s32[1]{0:T(128)} %bitcast.place_ref, s32[2048]{0:T(1024)S(1)} %add.7.code_ref, s32[16,128]{1,0:T(8,128)S(1)} %own_fill.1.fill_ref, f32[2048,128]{1,0:T(8,128)S(1)} %select_select_fusion.residual_ref, bf16[576,128]{1,0:T(8,128)(2,1)S(1)} %pad_maximum_fusion.rest_0_, ...), custom_call_target="tpu_custom_call" | custom-call | tf_op jit(solution)/shard_map/tile_maxima/pallas_call | solution.py:213
  35.1 4.1 %all-to-all-start = ((f32[16,8,128]{2,1,0:T(8,128)}), f32[16,8,128]{2,1,0:T(8,128)S(1)}, u32[]{:S(2)}, u32[]{:S(2)}) async-start(f32[16,8,128]{2,1,0:T(8,128)} %tile_maxima.1), calls=%async_computation | async-start | bytes 131072 | tf_op jit(solution)/shard_map/all_to_all | solution.py:332
  39.2 0.4 tile_starts.1
  39.6 6.5 %all-to-all-done.maxima_ref = f32[16,8,128]{2,1,0:T(8,128)S(1)} async-done(((f32[16,8,128]{2,1,0:T(8,128)}), f32[16,8,128]{2,1,0:T(8,128)S(1)}, u32[]{:S(2)}, u32[]{:S(2)}) %all-to-all-start) | async-done | bytes 65568 | tf_op jit(solution)/shard_map/all_to_all | solution.py:332
  46.1 0.9 %assemble.1 = f32[2,512]{1,0:T(2,128)} custom-call(f32[16,8,128]{2,1,0:T(8,128)S(1)} %all-to-all-done.maxima_ref, s32[256,128]{1,0:T(8,128)S(1)} %get-tuple-element.21.more_ref, s32[2,128]{1,0:T(2,128)S(1)} %get-tuple-element.22.start_ref, s32[2,512]{1,0:T(2,128)S(1)} %copy-done), custom_call_target="tpu_custom_call" | custom-call | tf_op jit(solution)/shard_map/assemble/pallas_call | solution.py:292
  (30 shorter events, 0.3 us)
Async XLA Ops:
  0.0 8.7 %copy-start.3 = (f32[4,128]{1,0:T(4,128)S(1)}, f32[4,128]{1,0:T(4,128)}, u32[]{:S(2)}) copy-start(f32[4,128]{1,0:T(4,128)} %param.12) | copy-start | bytes 6148
  1.0 16.3 %collective-permute-start.7 = (bf16[576,128]{1,0:T(8,128)(2,1)S(1)}, bf16[576,128]{1,0:T(8,128)(2,1)S(1)}, u32[]{:S(2)}, u32[]{:S(2)}) collective-permute-start(bf16[576,128]{1,0:T(8,128)(2,1)S(1)} %pad_maximum_fusion.rest_0_), channel_id=1, source_target_pairs={{0,1},{1,0},{2,3},{3,2},{4,5},{5,4},{6,7},{7,6},{8,9},{9,8},{10,11... | collective-permute-start | bytes 442376 | tf_op jit(solution)/shard_map/ppermute | solution.py:19
  1.5 19.3 %collective-permute-start.4 = (bf16[576,128]{1,0:T(8,128)(2,1)S(1)}, bf16[576,128]{1,0:T(8,128)(2,1)S(1)}, u32[]{:S(2)}, u32[]{:S(2)}) collective-permute-start(bf16[576,128]{1,0:T(8,128)(2,1)S(1)} %pad_maximum_fusion.rest_0_), channel_id=1, source_target_pairs={{0,4},{1,5},{2,6},{3,7},{4,0},{5,1},{6,2},{7,3},{8,12},{9,13},{10,... | collective-permute-start | bytes 442376 | tf_op jit(solution)/shard_map/ppermute | solution.py:19
  4.1 16.7 %collective-permute-start.3 = (bf16[576,128]{1,0:T(8,128)(2,1)S(1)}, bf16[576,128]{1,0:T(8,128)(2,1)S(1)}, u32[]{:S(2)}, u32[]{:S(2)}) collective-permute-start(bf16[576,128]{1,0:T(8,128)(2,1)S(1)} %pad_maximum_fusion.rest_0_), channel_id=1, source_target_pairs={{0,6},{1,7},{2,4},{3,5},{4,2},{5,3},{6,0},{7,1},{8,14},{9,15},{10,... | collective-permute-start | bytes 442376 | tf_op jit(solution)/shard_map/ppermute | solution.py:19
  5.6 16.8 %collective-permute-start.2 = (bf16[576,128]{1,0:T(8,128)(2,1)S(1)}, bf16[576,128]{1,0:T(8,128)(2,1)S(1)}, u32[]{:S(2)}, u32[]{:S(2)}) collective-permute-start(bf16[576,128]{1,0:T(8,128)(2,1)S(1)} %pad_maximum_fusion.rest_0_), channel_id=1, source_target_pairs={{0,2},{1,3},{2,0},{3,1},{4,6},{5,7},{6,4},{7,5},{8,10},{9,11},{10,... | collective-permute-start | bytes 442376 | tf_op jit(solution)/shard_map/ppermute | solution.py:19
  5.7 8.6 %collective-permute-start = (bf16[576,128]{1,0:T(8,128)(2,1)S(1)}, bf16[576,128]{1,0:T(8,128)(2,1)S(1)}, u32[]{:S(2)}, u32[]{:S(2)}) collective-permute-start(bf16[576,128]{1,0:T(8,128)(2,1)S(1)} %pad_maximum_fusion.rest_0_), channel_id=1, source_target_pairs={{0,8},{1,9},{2,10},{3,11},{4,12},{5,13},{6,14},{7,15},{8,0},{9,1},... | collective-permute-start | bytes 442376 | tf_op jit(solution)/shard_map/ppermute | solution.py:19
  14.3 6.6 %collective-permute-start.1 = (bf16[576,128]{1,0:T(8,128)(2,1)S(1)}, bf16[576,128]{1,0:T(8,128)(2,1)S(1)}, u32[]{:S(2)}, u32[]{:S(2)}) collective-permute-start(bf16[576,128]{1,0:T(8,128)(2,1)S(1)} %collective-permute-done.rest_1_), channel_id=1, source_target_pairs={{0,2},{1,3},{2,0},{3,1},{4,6},{5,7},{6,4},{7,5},{8,10},{9,11},{10,... | collective-permute-start | bytes 442376 | tf_op jit(solution)/shard_map/ppermute | solution.py:19
  15.8 5.6 %copy-start.2 = (s32[2048,1]{0,1:T(1,128)S(1)}, s32[2048,1]{0,1:T(1,128)}, u32[]{:S(2)}) copy-start(s32[2048,1]{0,1:T(1,128)} %param.13) | copy-start | bytes 24580
  17.2 4.2 %copy-start.1 = (s32[2048]{0:T(1024)S(1)}, s32[2048]{0:T(1024)}, u32[]{:S(2)}) copy-start(s32[2048]{0:T(1024)} %param.14) | copy-start | bytes 24580
  17.3 8.2 %collective-permute-start.6 = (bf16[576,128]{1,0:T(8,128)(2,1)S(1)}, bf16[576,128]{1,0:T(8,128)(2,1)S(1)}, u32[]{:S(2)}, u32[]{:S(2)}) collective-permute-start(bf16[576,128]{1,0:T(8,128)(2,1)S(1)} %collective-permute-done.rest_1_), channel_id=1, source_target_pairs={{0,4},{1,5},{2,6},{3,7},{4,0},{5,1},{6,2},{7,3},{8,12},{9,13},{10,... | collective-permute-start | bytes 442376 | tf_op jit(solution)/shard_map/ppermute | solution.py:19
  20.8 6.4 %collective-permute-start.5 = (bf16[576,128]{1,0:T(8,128)(2,1)S(1)}, bf16[576,128]{1,0:T(8,128)(2,1)S(1)}, u32[]{:S(2)}, u32[]{:S(2)}) collective-permute-start(bf16[576,128]{1,0:T(8,128)(2,1)S(1)} %collective-permute-done.rest_1_), channel_id=1, source_target_pairs={{0,6},{1,7},{2,4},{3,5},{4,2},{5,3},{6,0},{7,1},{8,14},{9,15},{10,... | collective-permute-start | bytes 442376 | tf_op jit(solution)/shard_map/ppermute | solution.py:19
  20.8 1.7 %collective-permute-start.11 = (bf16[576,128]{1,0:T(8,128)(2,1)S(1)}, bf16[576,128]{1,0:T(8,128)(2,1)S(1)}, u32[]{:S(2)}, u32[]{:S(2)}) collective-permute-start(bf16[576,128]{1,0:T(8,128)(2,1)S(1)} %collective-permute-done.4.rest_4_), channel_id=1, source_target_pairs={{0,1},{1,0},{2,3},{3,2},{4,5},{5,4},{6,7},{7,6},{8,9},{9,8},{10,11... | collective-permute-start | bytes 442376 | tf_op jit(solution)/shard_map/ppermute | solution.py:19
  20.9 6.3 %collective-permute-start.10 = (bf16[576,128]{1,0:T(8,128)(2,1)S(1)}, bf16[576,128]{1,0:T(8,128)(2,1)S(1)}, u32[]{:S(2)}, u32[]{:S(2)}) collective-permute-start(bf16[576,128]{1,0:T(8,128)(2,1)S(1)} %collective-permute-done.3.rest_3_), channel_id=1, source_target_pairs={{0,1},{1,0},{2,3},{3,2},{4,5},{5,4},{6,7},{7,6},{8,9},{9,8},{10,11... | collective-permute-start | bytes 442376 | tf_op jit(solution)/shard_map/ppermute | solution.py:19
  21.4 0.7 %copy-start.4 = (s32[160]{0:T(256)S(1)}, s32[160]{0:T(256)}, u32[]{:S(2)}) copy-start(s32[160]{0:T(256)} %param.17) | copy-start | bytes 1924
  21.4 0.7 %copy-start.5 = (s32[160]{0:T(256)S(1)}, s32[160]{0:T(256)}, u32[]{:S(2)}) copy-start(s32[160]{0:T(256)} %param.16) | copy-start | bytes 1924
  22.3 5.4 %collective-permute-start.8 = (bf16[576,128]{1,0:T(8,128)(2,1)S(1)}, bf16[576,128]{1,0:T(8,128)(2,1)S(1)}, u32[]{:S(2)}, u32[]{:S(2)}) collective-permute-start(bf16[576,128]{1,0:T(8,128)(2,1)S(1)} %collective-permute-done.rest_1_), channel_id=1, source_target_pairs={{0,1},{1,0},{2,3},{3,2},{4,5},{5,4},{6,7},{7,6},{8,9},{9,8},{10,11... | collective-permute-start | bytes 442376 | tf_op jit(solution)/shard_map/ppermute | solution.py:19
  22.5 5.2 %collective-permute-start.9 = (bf16[576,128]{1,0:T(8,128)(2,1)S(1)}, bf16[576,128]{1,0:T(8,128)(2,1)S(1)}, u32[]{:S(2)}, u32[]{:S(2)}) collective-permute-start(bf16[576,128]{1,0:T(8,128)(2,1)S(1)} %collective-permute-done.2.rest_2_), channel_id=1, source_target_pairs={{0,1},{1,0},{2,3},{3,2},{4,5},{5,4},{6,7},{7,6},{8,9},{9,8},{10,11... | collective-permute-start | bytes 442376 | tf_op jit(solution)/shard_map/ppermute | solution.py:19
  25.5 2.2 %collective-permute-start.14 = (bf16[576,128]{1,0:T(8,128)(2,1)S(1)}, bf16[576,128]{1,0:T(8,128)(2,1)S(1)}, u32[]{:S(2)}, u32[]{:S(2)}) collective-permute-start(bf16[576,128]{1,0:T(8,128)(2,1)S(1)} %collective-permute-done.6.rest_7_), channel_id=1, source_target_pairs={{0,1},{1,0},{2,3},{3,2},{4,5},{5,4},{6,7},{7,6},{8,9},{9,8},{10,11... | collective-permute-start | bytes 442376 | tf_op jit(solution)/shard_map/ppermute | solution.py:19
  27.2 1.4 %collective-permute-start.13 = (bf16[576,128]{1,0:T(8,128)(2,1)S(1)}, bf16[576,128]{1,0:T(8,128)(2,1)S(1)}, u32[]{:S(2)}, u32[]{:S(2)}) collective-permute-start(bf16[576,128]{1,0:T(8,128)(2,1)S(1)} %collective-permute-done.5.rest_6_), channel_id=1, source_target_pairs={{0,1},{1,0},{2,3},{3,2},{4,5},{5,4},{6,7},{7,6},{8,9},{9,8},{10,11... | collective-permute-start | bytes 442376 | tf_op jit(solution)/shard_map/ppermute | solution.py:19
  27.2 1.6 %collective-permute-start.12 = (bf16[576,128]{1,0:T(8,128)(2,1)S(1)}, bf16[576,128]{1,0:T(8,128)(2,1)S(1)}, u32[]{:S(2)}, u32[]{:S(2)}) collective-permute-start(bf16[576,128]{1,0:T(8,128)(2,1)S(1)} %collective-permute-done.1.rest_5_), channel_id=1, source_target_pairs={{0,1},{1,0},{2,3},{3,2},{4,5},{5,4},{6,7},{7,6},{8,9},{9,8},{10,11... | collective-permute-start | bytes 442376 | tf_op jit(solution)/shard_map/ppermute | solution.py:19
  35.1 11.0 %all-to-all-start = ((f32[16,8,128]{2,1,0:T(8,128)}), f32[16,8,128]{2,1,0:T(8,128)S(1)}, u32[]{:S(2)}, u32[]{:S(2)}) async-start(f32[16,8,128]{2,1,0:T(8,128)} %tile_maxima.1), calls=%async_computation | async-start | bytes 131072 | tf_op jit(solution)/shard_map/all_to_all | solution.py:332
  39.2 6.9 %copy-start = (s32[2,512]{1,0:T(2,128)S(1)}, s32[2,512]{1,0:T(2,128)}, u32[]{:S(2)}) copy-start(s32[2,512]{1,0:T(2,128)} %candidate_ref.1) | copy-start | bytes 12292
where the time goes:
time: 47.2 us; the launch traced here: 47 us
  starting transfers between devices  18.4 us (39%)
  waiting for transfers between devices  17.5 us (37%)
  Pallas kernels  7.88 us (17%)
  other arithmetic  2.4 us (5%)
  local copies, waits for them, and re-layouts  0.7 us (1%)
    ppermute x15, starting transfers between devices, swap(): return lax.ppermute(x, 'psg', [(i, i ^ offset) for i in range(n)])  14.4 us
    ppermute x15, waiting for transfers between devices, swap(): return lax.ppermute(x, 'psg', [(i, i ^ offset) for i in range(n)])  11 us
    all_to_all x1, waiting for transfers between devices, per_device(): lax.all_to_all(maxima, 'psg', split_axis=0, concat_axis=0, tiled=True)  6.48 us
    pallas_call x1, Pallas kernels, tile_maxima(): pl.pallas_call(functools.partial(maxima_kernel, names, query_rows), out_s...  6.32 us
    all_to_all x1, starting transfers between devices, per_device(): lax.all_to_all(maxima, 'psg', split_axis=0, concat_axis=0, tiled=True)  4.07 us
    select_n x1, other arithmetic, per_device(): jnp.where(residual_codes < 2, jnp.where(residual_codes == 0, bucket_weigh...  1.45 us
    concatenate x1, other arithmetic, per_device(): own = jnp.concatenate([centroids, queries.reshape(query_rows, dim)])  0.94 us
    pallas_call x1, Pallas kernels, assemble(): pl.pallas_call(functools.partial(assemble_kernel, query_len), out_shape=j...  0.94 us
  transfers between devices with their start and end apart: 16, of which 6 were waited for; matrix products, arithmetic and copies ran while one was open for 3% of the time, Pallas kernels for 1%

commit v1 on v0

--- a/solution.py
+++ b/solution.py
@@ -23,23 +23,33 @@
     return [1 << k for k in reversed(range(n.bit_length() - 1))]
 
 
-def spread(own, beside):
+def flipped(n):
+    return n - n // 4
+
+
+def spread(book, queries, beside):
     bits = bits_of(lax.axis_size("psg"))
-    far, mid, low = bits[0], bits[1], bits[2]
-    held = {0: own}
-    held[far] = swap(own, far)
-    held[low] = swap(own, low)
-    held[mid ^ low] = swap(own, mid ^ low)
-    held[mid] = swap(own, mid)
-    held[far ^ low] = swap(held[far], low)
-    held[far ^ mid ^ low] = swap(held[far], mid ^ low)
-    held[far ^ mid] = swap(held[far], mid)
-    held[far ^ low], beside = lax.optimization_barrier((held[far ^ low], beside))
-    pieces = [((o,), array) for o, array in held.items()]
+    far, mid, low = bits[:3]
+    half = book.shape[0] // 2
+    far_book, far_queries = swap(book, far), swap(queries, far)
+    own = jnp.concatenate([book, queries])
+    taken = lax.dynamic_slice_in_dim(own, lax.axis_index("groups") * half, half, 0)
+    some = jnp.concatenate([taken, queries])
+    held = {(0, 0): own}
+    held[low, 0] = swap(own, low)
+    held[mid ^ low, 1] = swap(some, mid ^ low)
+    held[mid, 1] = swap(some, mid)
+    held[far, 0] = jnp.concatenate([far_book, far_queries])
+    for offset in (low, mid ^ low, mid):
+        held[far ^ offset, 0] = swap(held[far, 0], offset)
+    for offset in (mid ^ low, mid):
+        held[offset, 2] = lax.ppermute(held[offset, 1][:half], "groups", [(0, 1), (1, 0)])
+    held[far ^ low, 0], beside = lax.optimization_barrier((held[far ^ low, 0], beside))
+    pieces = [((segment,), array) for segment, array in held.items()]
     for bit in bits[3:]:
-        if len(pieces) > 8:
-            pieces = [(sum([o for o, _ in pieces], ()), jnp.concatenate([a for _, a in pieces]))]
-        pieces = pieces + [(tuple(o ^ bit for o in names), swap(array, bit)) for names, array in pieces]
+        if len(pieces) > 10:
+            pieces = [(sum([names for names, _ in pieces], ()), jnp.concatenate([a for _, a in pieces]))]
+        pieces = pieces + [(tuple((o ^ bit, part) for o, part in names), swap(array, bit)) for names, array in pieces]
     return pieces, beside
 
 
@@ -120,107 +130,128 @@
     )(counts)
 
 
-def maxima_kernel(names, query_rows, place_ref, code_ref, fill_ref, residual_ref, *rest):
-    pieces = rest[: len(names)]
-    out_ref, book_ref, query_ref, even_ref, odd_ref, embedded_ref = rest[len(names) :]
+def maxima_kernel(segments, place_ref, code_ref, fill_ref, residual_ref, *rest):
+    pieces = rest[: len(segments)]
+    out_ref, book_ref, query_ref, picked_ref, near_ref, rear_ref, best_ref = rest[len(segments) :]
     index = place_ref[0]
-    each = pieces[0].shape[0] // len(names[0])
-    cent_dev = each - query_rows
-    for offsets, piece in zip(names, pieces):
-        for k, offset in enumerate(offsets):
-            book_at = pl.multiple_of((index ^ offset) * cent_dev, cent_dev)
-            query_at = pl.multiple_of((index ^ offset) * query_rows, query_rows)
-            query_ref[pl.ds(query_at, query_rows), :] = piece[k * each + cent_dev : (k + 1) * each, :]
-
-            def expand(step, carry, piece=piece, start=k * each, book_at=book_at):
+    peers = out_ref.shape[0]
+    query_rows = query_ref.shape[0] // peers
+    cent_dev = book_ref.shape[0] // peers
+    group = place_ref[1]
+    for names, piece in zip(segments, pieces):
+        start = 0
+        for offset, part in names:
+            source = index ^ offset
+            rows = cent_dev // (2 if part else 1)
+            book_at = source * cent_dev
+            if part:
+                book_at = book_at + (group if part == 1 else 1 - group) * rows
+            book_at = pl.multiple_of(book_at, LANES)
+
+            def expand(step, carry, piece=piece, start=start, book_at=book_at):
                 at = pl.multiple_of(step * LANES, LANES)
-                rows = piece[pl.ds(start + at, LANES), :].astype(jnp.float32)
-                book_ref[pl.ds(book_at + at, LANES), :] = rows
+                values = piece[pl.ds(start + at, LANES), :].astype(jnp.float32)
+                book_ref[pl.ds(book_at + at, LANES), :] = values
                 return carry
 
-            lax.fori_loop(0, cent_dev // LANES, expand, 0, unroll=len(names) > 8)
+            lax.fori_loop(0, rows // LANES, expand, 0, unroll=len(segments) > 8)
+            start = start + rows
+            if part < 2:
+                query_at = pl.multiple_of(source * query_rows, query_rows)
+                query_ref[pl.ds(query_at, query_rows), :] = piece[start : start + query_rows, :]
+                start = start + query_rows
 
     tiles = residual_ref.shape[0] // TILE
+    half = tiles // 2
     slot = lax.broadcasted_iota(jnp.int32, (TILE, LANES), 0)
 
-    def pick(tile, into):
-        base = tile * TILE
-        for u in range(TILE):
-            into[u : u + 1, :] = book_ref[pl.ds(code_ref[base + u], 1), :]
-
-    def decode(tile, picked):
-        rows = pl.ds(pl.multiple_of(tile * TILE, TILE), TILE)
-        summed = picked[...] + residual_ref[rows, :]
+    def pick(first, count):
+        for u in range(first, first + count):
+            picked_ref[u : u + 1, :] = book_ref[pl.ds(code_ref[u], 1), :]
+
+    def decode(tile, into, first):
+        summed = picked_ref[tile * TILE : (tile + 1) * TILE, :] + residual_ref[tile * TILE : (tile + 1) * TILE, :]
         scale = lax.rsqrt(jnp.sum(summed * summed, axis=1, keepdims=True) + EPSILON)
         embedded = summed * scale
-        embedded = jnp.where(slot < fill_ref[pl.ds(tile, 1), :], embedded, embedded[0:1, :])
-        embedded_ref[rows, :] = embedded.astype(jnp.bfloat16)
-
-    pick(0, even_ref)
-
-    def pair(step, carry):
-        tile = 2 * step
-        pick(tile + 1, odd_ref)
-        decode(tile, even_ref)
-        pick(jnp.minimum(tile + 2, tiles - 1), even_ref)
-        decode(tile + 1, odd_ref)
-        return carry
-
-    lax.fori_loop(0, tiles // 2, pair, 0)
-
-    width = 2 * LANES
-    per = LANES // query_rows
-    deep = tiles // per
-    lane = lax.broadcasted_iota(jnp.int32, (deep, LANES), 1)
-
-    def score(step, carry):
+        embedded = jnp.where(slot < fill_ref[tile : tile + 1, :], embedded, embedded[0:1, :])
+        into[(tile - first) * TILE : (tile - first + 1) * TILE, :] = embedded.astype(jnp.bfloat16)
+
+    def maxima(embedded, step, between=None):
         q = query_ref[pl.ds(pl.multiple_of(step * width, width), width), :]
-        rows = []
-        for t in range(tiles):
+        found = []
+        for t in range(half):
             products = lax.dot_general(
-                embedded_ref[t * TILE : (t + 1) * TILE, :],
+                embedded[t * TILE : (t + 1) * TILE, :],
                 q,
                 (((1,), (1,)), ((), ())),
                 preferred_element_type=jnp.float32,
             )
-            rows.append(jnp.max(products, axis=0, keepdims=True))
-        best = jnp.concatenate(rows, axis=0)
+            found.append(jnp.max(products, axis=0, keepdims=True))
+            if between is not None:
+                between(t)
+        return jnp.concatenate(found, axis=0)
+
+    width = 2 * LANES
+    steps = query_ref.shape[0] // width
+    for tile in range(half):
+        pick(tile * TILE, TILE)
+        if tile:
+            decode(tile - 1, near_ref, 0)
+    pick(half * TILE, TILE)
+    decode(half - 1, near_ref, 0)
+
+    def beside(t, step):
+        done = (half + 1) * TILE + (step * half + t) * part
+        count = min(part, tiles * TILE - done)
+        if count <= 0:
+            return
+        pick(done, count)
+        if (done + count) % TILE == 0:
+            decode((done + count) // TILE - 2, rear_ref, half)
+
+    part = -(-(half - 1) * TILE // (min(steps, half // 2) * half) // 8) * 8
+    for step in range(steps):
+        best_ref[step] = maxima(near_ref, step, functools.partial(beside, step=step))
+    decode(tiles - 1, rear_ref, half)
+
+    lane = lax.broadcasted_iota(jnp.int32, (half, LANES), 1)
+
+    def late(step, carry):
+        first = best_ref[step]
+        second = maxima(rear_ref, step)
         for b in range(width // LANES):
-            block = best[:, b * LANES : (b + 1) * LANES]
-            for turn in range(per):
-                made = None
-                for g in range(per):
-                    part = block[g * deep : (g + 1) * deep, :]
-                    shift = (g - turn) * query_rows % LANES
-                    if shift:
-                        part = pltpu.roll(part, shift, 1)
-                    made = part if made is None else jnp.where(lane < g * query_rows, made, part)
-                out_ref[step * (width // query_rows) + b * per + turn] = made
+            one = first[:, b * LANES : (b + 1) * LANES]
+            two = second[:, b * LANES : (b + 1) * LANES]
+            peer = step * (width // query_rows) + 2 * b
+            out_ref[peer ^ flipped(peers)] = jnp.where(lane < query_rows, one, pltpu.roll(two, query_rows, 1))
+            out_ref[(peer + 1) ^ flipped(peers)] = jnp.where(lane < query_rows, pltpu.roll(one, query_rows, 1), two)
         return carry
 
-    lax.fori_loop(0, query_ref.shape[0] // width, score, 0)
-
-
-def tile_maxima(held, place, codes, fill, residual, query_rows):
+    lax.fori_loop(0, steps, late, 0)
+
+
+def tile_maxima(held, place, codes, fill, residual, cent_dev, query_rows):
     n = lax.axis_size("psg")
     tokens, dim = residual.shape
-    cent_dev = held[0][1].shape[0] // len(held[0][0]) - query_rows
-    per = LANES // query_rows
+    tiles = tokens // TILE
+    width = 2 * LANES
+    if lax.axis_size("groups") != 2 or cent_dev % (2 * LANES) or 2 * query_rows != LANES or tiles % 4 or n * query_rows % width:
+        raise ValueError("unsupported sizes")
     smem = pl.BlockSpec(memory_space=pltpu.SMEM)
     vmem = pl.BlockSpec(memory_space=pltpu.VMEM)
-    names = tuple(o for o, _ in held)
-    room = (n * (cent_dev * 6 + query_rows * 4) + tokens * 6) * dim + GRANT
+    room = (n * (cent_dev * 6 + query_rows * 4) + tokens * 10) * dim + GRANT
     return pl.pallas_call(
-        functools.partial(maxima_kernel, names, query_rows),
-        out_shape=jax.ShapeDtypeStruct((n, tokens // TILE // per, LANES), jnp.float32),
+        functools.partial(maxima_kernel, tuple(o for o, _ in held)),
+        out_shape=jax.ShapeDtypeStruct((n, tiles // 2, LANES), jnp.float32),
         in_specs=[smem, smem, vmem, vmem] + [vmem] * len(held),
         out_specs=vmem,
         scratch_shapes=[
             pltpu.VMEM((n * cent_dev, dim), jnp.float32),
             pltpu.VMEM((n * query_rows, dim), jnp.bfloat16),
-            pltpu.VMEM((TILE, dim), jnp.float32),
-            pltpu.VMEM((TILE, dim), jnp.float32),
-            pltpu.VMEM((tokens, dim), jnp.bfloat16),
+            pltpu.VMEM((tokens, dim), jnp.float32),
+            pltpu.VMEM((tokens // 2, dim), jnp.bfloat16),
+            pltpu.VMEM((tokens // 2, dim), jnp.bfloat16),
+            pltpu.VMEM((n * query_rows // width, tiles // 2, width), jnp.float32),
         ],
         compiler_params=pltpu.CompilerParams(vmem_limit_bytes=room),
         name="tile_maxima",
@@ -244,7 +275,7 @@
     per = LANES // query_rows
     total = n * deep * per
     for j in range(n):
-        got = maxima_ref[j]
+        got = maxima_ref[j ^ flipped(n)]
         for g in range(per):
             at = (j * per + g) * deep
             part = got if g == 0 else pltpu.roll(got, LANES - g * query_rows, 1)
@@ -312,7 +343,7 @@
     last_fill,
 ):
     n = lax.axis_size("psg")
-    place = lax.axis_index("psg").astype(jnp.int32).reshape(1)
+    place = jnp.stack([lax.axis_index("psg"), lax.axis_index("groups")]).astype(jnp.int32)
     num_queries, query_len, dim = queries.shape
     tiles_dev = residual_codes.shape[0] // TILE
     counts, lasts = in_blocks(tile_count), in_blocks(last_fill)
@@ -324,12 +355,15 @@
     )
     fill = own_fill(place, counts, lasts, tiles_dev)
     query_rows = num_queries * query_len
-    own = jnp.concatenate([centroids, queries.reshape(query_rows, dim)])
-    held, (codes, fill, counts, residual) = spread(own, (codes, fill, counts, residual))
-    maxima = tile_maxima(held, place, codes, fill, residual, query_rows)
+    held, (codes, fill, counts, residual) = spread(
+        centroids, queries.reshape(query_rows, dim), (codes, fill, counts, residual)
+    )
+    maxima = tile_maxima(held, place, codes, fill, residual, centroids.shape[0], query_rows)
     maxima, counts = lax.optimization_barrier((maxima, counts))
     starts, more = tile_starts(counts, tiles_dev * n)
-    own_maxima = lax.all_to_all(maxima, "psg", split_axis=0, concat_axis=0, tiled=True)
+    own_maxima = lax.all_to_all(
+        maxima, "psg", split_axis=0, concat_axis=0, tiled=True, axis_index_groups=[[k ^ flipped(n) for k in range(n)]]
+    )
     return assemble(own_maxima, more, starts, candidates, query_len)
 
 

time: 47.2 us -> 46 us (0.975)
  waiting for transfers between devices: 17.5 us -> 12 us
  starting transfers between devices: 18.4 us -> 23.5 us
  local copies, waits for them, and re-layouts: 0.7 us -> 0.1 us
  Pallas kernels: 7.88 us -> 7.33 us
    ppermute x15 -> x18, waiting for transfers between devices: 11 us -> 6.78 us  [swap(): return lax.ppermute(x, 'psg', [(i, i ^ offset) for i in range(n)])]
    all_to_all x1, waiting for transfers between devices: 6.48 us -> 3.28 us  [per_device(): lax.all_to_all(maxima, 'psg', split_axis=0, concat_axis=0, tiled=True, ax...]
    ppermute x0 -> x2, starting transfers between devices: none -> 2.98 us  [spread(): lax.ppermute(held[offset, 1][:half], 'groups', [(0, 1), (1, 0)])]
    ppermute x0 -> x2, waiting for transfers between devices: none -> 1.95 us  [spread(): lax.ppermute(held[offset, 1][:half], 'groups', [(0, 1), (1, 0)])]
    all_to_all x1, starting transfers between devices: 4.07 us -> 5.28 us  [per_device(): lax.all_to_all(maxima, 'psg', split_axis=0, concat_axis=0, tiled=True, ax...]
    pallas_call x1, Pallas kernels: 6.32 us -> 5.23 us  [tile_maxima(): pl.pallas_call(functools.partial(maxima_kernel, tuple((o for o, _ in held...]
    ppermute x15 -> x18, starting transfers between devices: 14.4 us -> 15.3 us  [swap(): return lax.ppermute(x, 'psg', [(i, i ^ offset) for i in range(n)])]
    unnamed x12 -> x17, local copies, waits for them, and re-layouts: 0.69 us -> 0.07 us
  transfers between devices with their start and end apart: 16 -> 21, of which waited for: 6 -> 8; matrix products, arithmetic and copies ran while one was open for 3% -> 6% of each run, Pallas kernels for 1% -> 3%
where the time goes in v1:
time: 46 us; the launch traced here: 45.7 us
  starting transfers between devices  23.5 us (51%)
  waiting for transfers between devices  12 us (26%)
  Pallas kernels  7.33 us (16%)
  other arithmetic  2.5 us (5%)
    ppermute x18, starting transfers between devices, swap(): return lax.ppermute(x, 'psg', [(i, i ^ offset) for i in range(n)])  15.3 us
    ppermute x18, waiting for transfers between devices, swap(): return lax.ppermute(x, 'psg', [(i, i ^ offset) for i in range(n)])  6.78 us
    all_to_all x1, starting transfers between devices, per_device(): lax.all_to_all(maxima, 'psg', split_axis=0, concat_axis=0, tiled=True, ax...  5.28 us
    pallas_call x1, Pallas kernels, tile_maxima(): pl.pallas_call(functools.partial(maxima_kernel, tuple((o for o, _ in held...  5.23 us
    all_to_all x1, waiting for transfers between devices, per_device(): lax.all_to_all(maxima, 'psg', split_axis=0, concat_axis=0, tiled=True, ax...  3.28 us
    ppermute x2, starting transfers between devices, spread(): lax.ppermute(held[offset, 1][:half], 'groups', [(0, 1), (1, 0)])  2.98 us
    ppermute x2, waiting for transfers between devices, spread(): lax.ppermute(held[offset, 1][:half], 'groups', [(0, 1), (1, 0)])  1.95 us
    select_n x1, other arithmetic, per_device(): jnp.where(residual_codes < 2, jnp.where(residual_codes == 0, bucket_weigh...  1.43 us
  transfers between devices with their start and end apart: 21, of which 8 were waited for; matrix products, arithmetic and copies ran while one was open for 6% of the time, Pallas kernels for 3%

profile of v1, /device:TPU:0, one launch (start us, length us, event | category | flops | bytes accessed | tf_op | source)
XLA Modules:
  0.0 45.7 jit_solution(3290994965131551816)
XLA Ops:
  0.0 4.1 %collective-permute-start.1 = (bf16[64,128]{1,0:T(8,128)(2,1)}, bf16[64,128]{1,0:T(8,128)(2,1)S(1)}, u32[]{:S(2)}, u32[]{:S(2)}) collective-permute-start(bf16[64,128]{1,0:T(8,128)(2,1)} %bitcast.16), channel_id=1, source_target_pairs={{0,8},{1,9},{2,10},{3,11},{4,12},{5,13},{6,14},{7,15},{8,0},{9,1},... | collective-permute-start | bytes 49160 | tf_op jit(solution)/shard_map/ppermute | solution.py:19
  4.1 1.0 %fusion = bf16[256,128]{1,0:T(8,128)(2,1)S(1)} fusion(s32[]{:T(128)S(6)} %select_n.17, bf16[512,128]{1,0:T(8,128)(2,1)} %param.11, bf16[64,128]{1,0:T(8,128)(2,1)S(1)} %bitcast.17), kind=kLoop, calls=%fused_computation.5 | loop fusion | flops 131072 | bytes 212996 | tf_op jit(solution)/shard_map/concatenate | solution.py:35
  5.1 1.6 %collective-permute-start.5 = (bf16[320,128]{1,0:T(8,128)(2,1)S(1)}, bf16[320,128]{1,0:T(8,128)(2,1)S(1)}, u32[]{:S(2)}, u32[]{:S(2)}) collective-permute-start(bf16[320,128]{1,0:T(8,128)(2,1)S(1)} %pad_maximum_fusion.1), channel_id=1, source_target_pairs={{0,4},{1,5},{2,6},{3,7},{4,0},{5,1},{6,2},{7,3},{8,12},{9,13},{10,... | collective-permute-start | bytes 245768 | tf_op jit(solution)/shard_map/ppermute | solution.py:19
  6.7 1.4 %collective-permute-start.4 = (bf16[320,128]{1,0:T(8,128)(2,1)S(1)}, bf16[320,128]{1,0:T(8,128)(2,1)S(1)}, u32[]{:S(2)}, u32[]{:S(2)}) collective-permute-start(bf16[320,128]{1,0:T(8,128)(2,1)S(1)} %pad_maximum_fusion.1), channel_id=1, source_target_pairs={{0,6},{1,7},{2,4},{3,5},{4,2},{5,3},{6,0},{7,1},{8,14},{9,15},{10,... | collective-permute-start | bytes 245768 | tf_op jit(solution)/shard_map/ppermute | solution.py:19
  8.1 0.7 %collective-permute-start = (bf16[512,128]{1,0:T(8,128)(2,1)S(1)}, bf16[512,128]{1,0:T(8,128)(2,1)S(1)}, u32[]{:S(2)}, u32[]{:S(2)}) collective-permute-start(bf16[512,128]{1,0:T(8,128)(2,1)S(1)} %copy-done.1), channel_id=1, source_target_pairs={{0,8},{1,9},{2,10},{3,11},{4,12},{5,13},{6,14},{7,15},{8,0},{9,1},... | collective-permute-start | bytes 393224 | tf_op jit(solution)/shard_map/ppermute | solution.py:19
  9.0 1.4 %select_select_fusion.residual_ref = f32[2048,128]{1,0:T(8,128)S(1)} fusion(s32[2048,128]{1,0:T(8,128)} %param.15, f32[128]{0:T(128)S(1)} %get-tuple-element.25, f32[128]{0:T(128)S(1)} %get-tuple-element.26, f32[128]{0:T(128)S(1)} %get-tuple-element.24, f32[128]{0:T(128)S(1)} %get-tuple-element.23), kind=kLoop, calls=%fused_computation | loop fusion | flops 1572864 | bytes 2099200 | tf_op jit(solution)/shard_map/jit(_where)/select_n | solution.py:351
  10.4 2.9 %collective-permute-start.3 = (bf16[576,128]{1,0:T(8,128)(2,1)S(1)}, bf16[576,128]{1,0:T(8,128)(2,1)S(1)}, u32[]{:S(2)}, u32[]{:S(2)}) collective-permute-start(bf16[576,128]{1,0:T(8,128)(2,1)S(1)} %pad_maximum_fusion.rest_0_), channel_id=1, source_target_pairs={{0,2},{1,3},{2,0},{3,1},{4,6},{5,7},{6,4},{7,5},{8,10},{9,11},{10,... | collective-permute-start | bytes 442376 | tf_op jit(solution)/shard_map/ppermute | solution.py:19
  13.3 0.7 %collective-permute-done.4.rest_2_ = bf16[320,128]{1,0:T(8,128)(2,1)S(1)} collective-permute-done((bf16[320,128]{1,0:T(8,128)(2,1)S(1)}, bf16[320,128]{1,0:T(8,128)(2,1)S(1)}, u32[]{:S(2)}, u32[]{:S(2)}) %collective-permute-start.4) | collective-permute-done | bytes 81952 | tf_op jit(solution)/shard_map/ppermute | solution.py:19
  14.0 1.5 %collective-permute-start.9 = (bf16[256,128]{1,0:T(8,128)(2,1)S(1)}, bf16[256,128]{1,0:T(8,128)(2,1)S(1)}, u32[]{:S(2)}, u32[]{:S(2)}) collective-permute-start(bf16[256,128]{1,0:T(8,128)(2,1)S(1)} %slice.25), channel_id=1, source_target_pairs={{0,16},{16,0},{1,17},{17,1},{2,18},{18,2},{3,19},{19,3},{4,20},{20... | collective-permute-start | bytes 196616 | tf_op jit(solution)/shard_map/ppermute | solution.py:46
  15.5 0.8 %collective-permute-done = bf16[512,128]{1,0:T(8,128)(2,1)S(1)} collective-permute-done((bf16[512,128]{1,0:T(8,128)(2,1)S(1)}, bf16[512,128]{1,0:T(8,128)(2,1)S(1)}, u32[]{:S(2)}, u32[]{:S(2)}) %collective-permute-start) | collective-permute-done | bytes 131104 | tf_op jit(solution)/shard_map/ppermute | solution.py:19
  16.3 1.5 %collective-permute-start.8 = (bf16[256,128]{1,0:T(8,128)(2,1)S(1)}, bf16[256,128]{1,0:T(8,128)(2,1)S(1)}, u32[]{:S(2)}, u32[]{:S(2)}) collective-permute-start(bf16[256,128]{1,0:T(8,128)(2,1)S(1)} %slice.24), channel_id=1, source_target_pairs={{0,16},{16,0},{1,17},{17,1},{2,18},{18,2},{3,19},{19,3},{4,20},{20... | collective-permute-start | bytes 196616 | tf_op jit(solution)/shard_map/ppermute | solution.py:46
  17.9 0.6 %collective-permute-start.2 = (bf16[576,128]{1,0:T(8,128)(2,1)S(1)}, bf16[576,128]{1,0:T(8,128)(2,1)S(1)}, u32[]{:S(2)}, u32[]{:S(2)}) collective-permute-start(bf16[576,128]{1,0:T(8,128)(2,1)S(1)} %constant_dynamic-update-slice_fusion.rest_4_), channel_id=1, source_target_pairs={{0,2},{1,3},{2,0},{3,1},{4,6},{5,7},{6,4},{7,5},{8,10},{9,11},{10,... | collective-permute-start | bytes 442376 | tf_op jit(solution)/shard_map/ppermute | solution.py:19
  18.6 1.9 %collective-permute-done.8.rest_8_ = bf16[256,128]{1,0:T(8,128)(2,1)S(1)} collective-permute-done((bf16[256,128]{1,0:T(8,128)(2,1)S(1)}, bf16[256,128]{1,0:T(8,128)(2,1)S(1)}, u32[]{:S(2)}, u32[]{:S(2)}) %collective-permute-start.8) | collective-permute-done | bytes 65568 | tf_op jit(solution)/shard_map/ppermute | solution.py:46
  20.6 2.0 %collective-permute-start.6 = (bf16[576,128]{1,0:T(8,128)(2,1)S(1)}, bf16[576,128]{1,0:T(8,128)(2,1)S(1)}, u32[]{:S(2)}, u32[]{:S(2)}) collective-permute-start(bf16[576,128]{1,0:T(8,128)(2,1)S(1)} %constant_dynamic-update-slice_fusion.rest_4_), channel_id=1, source_target_pairs={{0,6},{1,7},{2,4},{3,5},{4,2},{5,3},{6,0},{7,1},{8,14},{9,15},{10,... | collective-permute-start | bytes 442376 | tf_op jit(solution)/shard_map/ppermute | solution.py:19
  22.7 0.5 %collective-permute-start.19 = (bf16[256,128]{1,0:T(8,128)(2,1)S(1)}, bf16[256,128]{1,0:T(8,128)(2,1)S(1)}, u32[]{:S(2)}, u32[]{:S(2)}) collective-permute-start(bf16[256,128]{1,0:T(8,128)(2,1)S(1)} %collective-permute-done.9.rest_9_), channel_id=1, source_target_pairs={{0,1},{1,0},{2,3},{3,2},{4,5},{5,4},{6,7},{7,6},{8,9},{9,8},{10,11... | collective-permute-start | bytes 196616 | tf_op jit(solution)/shard_map/ppermute | solution.py:19
  23.4 0.8 %own_fill.1.fill_ref = s32[16,128]{1,0:T(8,128)S(1)} custom-call(s32[2]{0:T(128)S(1)} %pad_add_fusion.place_ref, s32[2,128]{1,0:T(2,128)S(1)} %get-tuple-element.20.count_ref, s32[2,128]{1,0:T(2,128)S(1)} %get-tuple-element.27.last_ref), custom_call_target="tpu_custom_call" | custom-call | tf_op jit(solution)/shard_map/own_fill/pallas_call | solution.py:108
  24.7 1.7 %collective-permute-done.7.rest_7_ = bf16[576,128]{1,0:T(8,128)(2,1)S(1)} collective-permute-done((bf16[576,128]{1,0:T(8,128)(2,1)S(1)}, bf16[576,128]{1,0:T(8,128)(2,1)S(1)}, u32[]{:S(2)}, u32[]{:S(2)}) %collective-permute-start.7) | collective-permute-done | bytes 147488 | tf_op jit(solution)/shard_map/ppermute | solution.py:19
  26.5 2.5 %collective-permute-done.6.rest_6_ = bf16[576,128]{1,0:T(8,128)(2,1)S(1)} collective-permute-done((bf16[576,128]{1,0:T(8,128)(2,1)S(1)}, bf16[576,128]{1,0:T(8,128)(2,1)S(1)}, u32[]{:S(2)}, u32[]{:S(2)}) %collective-permute-start.6) | collective-permute-done | bytes 147488 | tf_op jit(solution)/shard_map/ppermute | solution.py:19
  29.0 0.5 %collective-permute-start.15 = (bf16[576,128]{1,0:T(8,128)(2,1)S(1)}, bf16[576,128]{1,0:T(8,128)(2,1)S(1)}, u32[]{:S(2)}, u32[]{:S(2)}) collective-permute-start(bf16[576,128]{1,0:T(8,128)(2,1)S(1)} %collective-permute-done.2.rest_5_), channel_id=1, source_target_pairs={{0,1},{1,0},{2,3},{3,2},{4,5},{5,4},{6,7},{7,6},{8,9},{9,8},{10,11... | collective-permute-start | bytes 442376 | tf_op jit(solution)/shard_map/ppermute | solution.py:19
  29.5 0.8 %collective-permute-done.16.rest_16_ = bf16[576,128]{1,0:T(8,128)(2,1)S(1)} collective-permute-done((bf16[576,128]{1,0:T(8,128)(2,1)S(1)}, bf16[576,128]{1,0:T(8,128)(2,1)S(1)}, u32[]{:S(2)}, u32[]{:S(2)}) %collective-permute-start.16) | collective-permute-done | bytes 147488 | tf_op jit(solution)/shard_map/ppermute | solution.py:19
  30.5 5.2 %tile_maxima.1 = f32[16,8,128]{2,1,0:T(8,128)} custom-call(s32[2]{0:T(128)S(1)} %pad_add_fusion.place_ref, s32[2048]{0:T(1024)S(1)} %add.10.code_ref, s32[16,128]{1,0:T(8,128)S(1)} %own_fill.1.fill_ref, f32[2048,128]{1,0:T(8,128)S(1)} %select_select_fusion.residual_ref, bf16[576,128]{1,0:T(8,128)(2,1)S(1)} %pad_maximum_fusion.rest_0_, ...), custom_call_target="tpu_custom_call" | custom-call | tf_op jit(solution)/shard_map/tile_maxima/pallas_call | solution.py:243
  35.8 5.3 %all-to-all-start = ((f32[16,8,128]{2,1,0:T(8,128)}), f32[16,8,128]{2,1,0:T(8,128)S(1)}, u32[]{:S(2)}, u32[]{:S(2)}) async-start(f32[16,8,128]{2,1,0:T(8,128)} %tile_maxima.1), calls=%async_computation | async-start | bytes 131072 | tf_op jit(solution)/shard_map/all_to_all | solution.py:364
  41.5 3.3 %all-to-all-done.maxima_ref = f32[16,8,128]{2,1,0:T(8,128)S(1)} async-done(((f32[16,8,128]{2,1,0:T(8,128)}), f32[16,8,128]{2,1,0:T(8,128)S(1)}, u32[]{:S(2)}, u32[]{:S(2)}) %all-to-all-start) | async-done | bytes 65568 | tf_op jit(solution)/shard_map/all_to_all | solution.py:364
  44.7 0.9 %assemble.1 = f32[2,512]{1,0:T(2,128)} custom-call(f32[16,8,128]{2,1,0:T(8,128)S(1)} %all-to-all-done.maxima_ref, s32[256,128]{1,0:T(8,128)S(1)} %get-tuple-element.21.more_ref, s32[2,128]{1,0:T(2,128)S(1)} %get-tuple-element.22.start_ref, s32[2,512]{1,0:T(2,128)S(1)} %copy-done), custom_call_target="tpu_custom_call" | custom-call | tf_op jit(solution)/shard_map/assemble/pallas_call | solution.py:323
  (51 shorter events, 1.7 us)
Async XLA Ops:
  0.0 17.8 %collective-permute-start.1 = (bf16[64,128]{1,0:T(8,128)(2,1)}, bf16[64,128]{1,0:T(8,128)(2,1)S(1)}, u32[]{:S(2)}, u32[]{:S(2)}) collective-permute-start(bf16[64,128]{1,0:T(8,128)(2,1)} %bitcast.16), channel_id=1, source_target_pairs={{0,8},{1,9},{2,10},{3,11},{4,12},{5,13},{6,14},{7,15},{8,0},{9,1},... | collective-permute-start | bytes 49160 | tf_op jit(solution)/shard_map/ppermute | solution.py:19
  5.1 5.3 %collective-permute-start.5 = (bf16[320,128]{1,0:T(8,128)(2,1)S(1)}, bf16[320,128]{1,0:T(8,128)(2,1)S(1)}, u32[]{:S(2)}, u32[]{:S(2)}) collective-permute-start(bf16[320,128]{1,0:T(8,128)(2,1)S(1)} %pad_maximum_fusion.1), channel_id=1, source_target_pairs={{0,4},{1,5},{2,6},{3,7},{4,0},{5,1},{6,2},{7,3},{8,12},{9,13},{10,... | collective-permute-start | bytes 245768 | tf_op jit(solution)/shard_map/ppermute | solution.py:19
  6.7 7.3 %collective-permute-start.4 = (bf16[320,128]{1,0:T(8,128)(2,1)S(1)}, bf16[320,128]{1,0:T(8,128)(2,1)S(1)}, u32[]{:S(2)}, u32[]{:S(2)}) collective-permute-start(bf16[320,128]{1,0:T(8,128)(2,1)S(1)} %pad_maximum_fusion.1), channel_id=1, source_target_pairs={{0,6},{1,7},{2,4},{3,5},{4,2},{5,3},{6,0},{7,1},{8,14},{9,15},{10,... | collective-permute-start | bytes 245768 | tf_op jit(solution)/shard_map/ppermute | solution.py:19
  8.1 8.2 %collective-permute-start = (bf16[512,128]{1,0:T(8,128)(2,1)S(1)}, bf16[512,128]{1,0:T(8,128)(2,1)S(1)}, u32[]{:S(2)}, u32[]{:S(2)}) collective-permute-start(bf16[512,128]{1,0:T(8,128)(2,1)S(1)} %copy-done.1), channel_id=1, source_target_pairs={{0,8},{1,9},{2,10},{3,11},{4,12},{5,13},{6,14},{7,15},{8,0},{9,1},... | collective-permute-start | bytes 393224 | tf_op jit(solution)/shard_map/ppermute | solution.py:19
  8.9 11.7 %collective-permute-start.10 = (bf16[576,128]{1,0:T(8,128)(2,1)S(1)}, bf16[576,128]{1,0:T(8,128)(2,1)S(1)}, u32[]{:S(2)}, u32[]{:S(2)}) collective-permute-start(bf16[576,128]{1,0:T(8,128)(2,1)S(1)} %pad_maximum_fusion.rest_0_), channel_id=1, source_target_pairs={{0,1},{1,0},{2,3},{3,2},{4,5},{5,4},{6,7},{7,6},{8,9},{9,8},{10,11... | collective-permute-start | bytes 442376 | tf_op jit(solution)/shard_map/ppermute | solution.py:19
  10.4 12.2 %collective-permute-start.3 = (bf16[576,128]{1,0:T(8,128)(2,1)S(1)}, bf16[576,128]{1,0:T(8,128)(2,1)S(1)}, u32[]{:S(2)}, u32[]{:S(2)}) collective-permute-start(bf16[576,128]{1,0:T(8,128)(2,1)S(1)} %pad_maximum_fusion.rest_0_), channel_id=1, source_target_pairs={{0,2},{1,3},{2,0},{3,1},{4,6},{5,7},{6,4},{7,5},{8,10},{9,11},{10,... | collective-permute-start | bytes 442376 | tf_op jit(solution)/shard_map/ppermute | solution.py:19
  14.0 4.5 %collective-permute-start.9 = (bf16[256,128]{1,0:T(8,128)(2,1)S(1)}, bf16[256,128]{1,0:T(8,128)(2,1)S(1)}, u32[]{:S(2)}, u32[]{:S(2)}) collective-permute-start(bf16[256,128]{1,0:T(8,128)(2,1)S(1)} %slice.25), channel_id=1, source_target_pairs={{0,16},{16,0},{1,17},{17,1},{2,18},{18,2},{3,19},{19,3},{4,20},{20... | collective-permute-start | bytes 196616 | tf_op jit(solution)/shard_map/ppermute | solution.py:46
  16.3 4.3 %collective-permute-start.8 = (bf16[256,128]{1,0:T(8,128)(2,1)S(1)}, bf16[256,128]{1,0:T(8,128)(2,1)S(1)}, u32[]{:S(2)}, u32[]{:S(2)}) collective-permute-start(bf16[256,128]{1,0:T(8,128)(2,1)S(1)} %slice.24), channel_id=1, source_target_pairs={{0,16},{16,0},{1,17},{17,1},{2,18},{18,2},{3,19},{19,3},{4,20},{20... | collective-permute-start | bytes 196616 | tf_op jit(solution)/shard_map/ppermute | solution.py:46
  17.9 4.8 %copy-start.6 = (s32[160]{0:T(256)S(1)}, s32[160]{0:T(256)}, u32[]{:S(2)}) copy-start(s32[160]{0:T(256)} %param.17) | copy-start | bytes 1924
  17.9 4.7 %copy-start.7 = (s32[160]{0:T(256)S(1)}, s32[160]{0:T(256)}, u32[]{:S(2)}) copy-start(s32[160]{0:T(256)} %param.16) | copy-start | bytes 1924
  17.9 5.4 %collective-permute-start.2 = (bf16[576,128]{1,0:T(8,128)(2,1)S(1)}, bf16[576,128]{1,0:T(8,128)(2,1)S(1)}, u32[]{:S(2)}, u32[]{:S(2)}) collective-permute-start(bf16[576,128]{1,0:T(8,128)(2,1)S(1)} %constant_dynamic-update-slice_fusion.rest_4_), channel_id=1, source_target_pairs={{0,2},{1,3},{2,0},{3,1},{4,6},{5,7},{6,4},{7,5},{8,10},{9,11},{10,... | collective-permute-start | bytes 442376 | tf_op jit(solution)/shard_map/ppermute | solution.py:19
  18.5 4.1 %copy-start.3 = (s32[2048]{0:T(1024)S(1)}, s32[2048]{0:T(1024)}, u32[]{:S(2)}) copy-start(s32[2048]{0:T(1024)} %param.14) | copy-start | bytes 24580
  18.6 4.2 %collective-permute-start.13 = (bf16[320,128]{1,0:T(8,128)(2,1)S(1)}, bf16[320,128]{1,0:T(8,128)(2,1)S(1)}, u32[]{:S(2)}, u32[]{:S(2)}) collective-permute-start(bf16[320,128]{1,0:T(8,128)(2,1)S(1)} %collective-permute-done.5.rest_3_), channel_id=1, source_target_pairs={{0,1},{1,0},{2,3},{3,2},{4,5},{5,4},{6,7},{7,6},{8,9},{9,8},{10,11... | collective-permute-start | bytes 245768 | tf_op jit(solution)/shard_map/ppermute | solution.py:19
  20.6 5.9 %collective-permute-start.7 = (bf16[576,128]{1,0:T(8,128)(2,1)S(1)}, bf16[576,128]{1,0:T(8,128)(2,1)S(1)}, u32[]{:S(2)}, u32[]{:S(2)}) collective-permute-start(bf16[576,128]{1,0:T(8,128)(2,1)S(1)} %constant_dynamic-update-slice_fusion.rest_4_), channel_id=1, source_target_pairs={{0,4},{1,5},{2,6},{3,7},{4,0},{5,1},{6,2},{7,3},{8,12},{9,13},{10,... | collective-permute-start | bytes 442376 | tf_op jit(solution)/shard_map/ppermute | solution.py:19
  20.6 8.3 %collective-permute-start.6 = (bf16[576,128]{1,0:T(8,128)(2,1)S(1)}, bf16[576,128]{1,0:T(8,128)(2,1)S(1)}, u32[]{:S(2)}, u32[]{:S(2)}) collective-permute-start(bf16[576,128]{1,0:T(8,128)(2,1)S(1)} %constant_dynamic-update-slice_fusion.rest_4_), channel_id=1, source_target_pairs={{0,6},{1,7},{2,4},{3,5},{4,2},{5,3},{6,0},{7,1},{8,14},{9,15},{10,... | collective-permute-start | bytes 442376 | tf_op jit(solution)/shard_map/ppermute | solution.py:19
  22.7 1.5 %collective-permute-start.12 = (bf16[320,128]{1,0:T(8,128)(2,1)S(1)}, bf16[320,128]{1,0:T(8,128)(2,1)S(1)}, u32[]{:S(2)}, u32[]{:S(2)}) collective-permute-start(bf16[320,128]{1,0:T(8,128)(2,1)S(1)} %collective-permute-done.4.rest_2_), channel_id=1, source_target_pairs={{0,1},{1,0},{2,3},{3,2},{4,5},{5,4},{6,7},{7,6},{8,9},{9,8},{10,11... | collective-permute-start | bytes 245768 | tf_op jit(solution)/shard_map/ppermute | solution.py:19
  22.7 1.9 %collective-permute-start.19 = (bf16[256,128]{1,0:T(8,128)(2,1)S(1)}, bf16[256,128]{1,0:T(8,128)(2,1)S(1)}, u32[]{:S(2)}, u32[]{:S(2)}) collective-permute-start(bf16[256,128]{1,0:T(8,128)(2,1)S(1)} %collective-permute-done.9.rest_9_), channel_id=1, source_target_pairs={{0,1},{1,0},{2,3},{3,2},{4,5},{5,4},{6,7},{7,6},{8,9},{9,8},{10,11... | collective-permute-start | bytes 196616 | tf_op jit(solution)/shard_map/ppermute | solution.py:19
  23.2 5.7 %collective-permute-start.18 = (bf16[256,128]{1,0:T(8,128)(2,1)S(1)}, bf16[256,128]{1,0:T(8,128)(2,1)S(1)}, u32[]{:S(2)}, u32[]{:S(2)}) collective-permute-start(bf16[256,128]{1,0:T(8,128)(2,1)S(1)} %collective-permute-done.8.rest_8_), channel_id=1, source_target_pairs={{0,1},{1,0},{2,3},{3,2},{4,5},{5,4},{6,7},{7,6},{8,9},{9,8},{10,11... | collective-permute-start | bytes 196616 | tf_op jit(solution)/shard_map/ppermute | solution.py:19
  24.2 5.3 %collective-permute-start.14 = (bf16[576,128]{1,0:T(8,128)(2,1)S(1)}, bf16[576,128]{1,0:T(8,128)(2,1)S(1)}, u32[]{:S(2)}, u32[]{:S(2)}) collective-permute-start(bf16[576,128]{1,0:T(8,128)(2,1)S(1)} %constant_dynamic-update-slice_fusion.rest_4_), channel_id=1, source_target_pairs={{0,1},{1,0},{2,3},{3,2},{4,5},{5,4},{6,7},{7,6},{8,9},{9,8},{10,11... | collective-permute-start | bytes 442376 | tf_op jit(solution)/shard_map/ppermute | solution.py:19
  24.7 4.8 %collective-permute-start.11 = (bf16[576,128]{1,0:T(8,128)(2,1)S(1)}, bf16[576,128]{1,0:T(8,128)(2,1)S(1)}, u32[]{:S(2)}, u32[]{:S(2)}) collective-permute-start(bf16[576,128]{1,0:T(8,128)(2,1)S(1)} %collective-permute-done.3.rest_1_), channel_id=1, source_target_pairs={{0,1},{1,0},{2,3},{3,2},{4,5},{5,4},{6,7},{7,6},{8,9},{9,8},{10,11... | collective-permute-start | bytes 442376 | tf_op jit(solution)/shard_map/ppermute | solution.py:19
  26.5 3.0 %collective-permute-start.17 = (bf16[576,128]{1,0:T(8,128)(2,1)S(1)}, bf16[576,128]{1,0:T(8,128)(2,1)S(1)}, u32[]{:S(2)}, u32[]{:S(2)}) collective-permute-start(bf16[576,128]{1,0:T(8,128)(2,1)S(1)} %collective-permute-done.7.rest_7_), channel_id=1, source_target_pairs={{0,1},{1,0},{2,3},{3,2},{4,5},{5,4},{6,7},{7,6},{8,9},{9,8},{10,11... | collective-permute-start | bytes 442376 | tf_op jit(solution)/shard_map/ppermute | solution.py:19
  28.9 1.4 %collective-permute-start.16 = (bf16[576,128]{1,0:T(8,128)(2,1)S(1)}, bf16[576,128]{1,0:T(8,128)(2,1)S(1)}, u32[]{:S(2)}, u32[]{:S(2)}) collective-permute-start(bf16[576,128]{1,0:T(8,128)(2,1)S(1)} %collective-permute-done.6.rest_6_), channel_id=1, source_target_pairs={{0,1},{1,0},{2,3},{3,2},{4,5},{5,4},{6,7},{7,6},{8,9},{9,8},{10,11... | collective-permute-start | bytes 442376 | tf_op jit(solution)/shard_map/ppermute | solution.py:19
  29.0 1.6 %collective-permute-start.15 = (bf16[576,128]{1,0:T(8,128)(2,1)S(1)}, bf16[576,128]{1,0:T(8,128)(2,1)S(1)}, u32[]{:S(2)}, u32[]{:S(2)}) collective-permute-start(bf16[576,128]{1,0:T(8,128)(2,1)S(1)} %collective-permute-done.2.rest_5_), channel_id=1, source_target_pairs={{0,1},{1,0},{2,3},{3,2},{4,5},{5,4},{6,7},{7,6},{8,9},{9,8},{10,11... | collective-permute-start | bytes 442376 | tf_op jit(solution)/shard_map/ppermute | solution.py:19
  35.8 9.0 %all-to-all-start = ((f32[16,8,128]{2,1,0:T(8,128)}), f32[16,8,128]{2,1,0:T(8,128)S(1)}, u32[]{:S(2)}, u32[]{:S(2)}) async-start(f32[16,8,128]{2,1,0:T(8,128)} %tile_maxima.1), calls=%async_computation | async-start | bytes 131072 | tf_op jit(solution)/shard_map/all_to_all | solution.py:364
  (5 other events, 15.4 us)
